TPU v7x, 32 devices: a whole 2x2x4 slice. The times are simulated.
32 devices in a mesh: groups: 2 (over y), tile: 8 (over z, x), band: 2 (over core).
Axes of the slice: x: 2, y: 2, z: 4, core: 2. Of those that a mesh axis runs over, the one named last changes fastest.
Arguments:
- cube: bfloat16 [128, 128, 1024], P(('groups', 'band'), None, 'tile'), parts along dimension 0, may hold values from -6 to 6
- kernels: bfloat16 [32, 64, 192], replicated, may hold values from -0.0546875 to 0.0546875
- zone_map: int32 [16, 128], P(None, 'tile'), may hold values from 0 to 3
- kernel_index: int32 [64, 4], replicated, may hold values from 0 to 31
- measurement: float32 [256, 1024], P(('groups', 'tile', 'band')), parts along dimension 0, may hold values from -6 to 6
- step_size: float32 [64], P('band'), may hold values from 1 to 4
- spectral_weight: float32 [64], P('band'), may hold values from 0.05 to 0.3
- prior_taps: float32 [3, 3], replicated, may hold values from -0.6 to 0.6
Outputs:
- updated: bfloat16 [128, 128, 1024], P(('groups', 'band'), None, 'tile'), parts along dimension 0
- residual: float32 [256, 1024], P(('groups', 'tile', 'band')), parts along dimension 0
There are 2 independent parts, one for each index of `groups`. A program takes and returns all parts, laid end to end along the dimension named above; an argument that names none is the same for every part. Nothing has to cross between parts.
Inputs may be any that keep to these rules, and one draw needn't show every extreme that they name: `kernel_index`: row of the kernel table.
All inputs are finite; a program needn't handle non-finite values.
Results may differ from a plain program's by a relative error of at most 0.0031.
Values may be sent and summed in bfloat16 or wider, within the bound.
A program may use at most 128 MiB of HBM per device.

v0:
```python
import functools

import jax
import jax.numpy as jnp
from jax import lax
from jax.experimental import pallas as pl
from jax.experimental.pallas import tpu as pltpu
from jax.sharding import PartitionSpec as P

BLOCK = 8
SUP = 3
ZONES = 4
PIX = BLOCK * BLOCK
F32 = jnp.float32
BF16 = jnp.bfloat16
MESH = pl.DeviceIdType.MESH
NT = (((1,), (1,)), ((), ()))


def iota(shape, dim):
    return lax.broadcasted_iota(jnp.int32, shape, dim)


def onehot(mask):
    return jnp.where(mask, 1.0, 0.0).astype(BF16)


def dot(a, b):
    return jnp.dot(a, b, preferred_element_type=F32)


def dot_nt(a, b):
    return lax.dot_general(a, b, NT, preferred_element_type=F32)


def kernel(
    tiles,
    cube_ref, kern_ref, zone_ref, meas_ref, kidx_ref, step_ref, weight_ref, taps_ref,
    out_ref, res_ref,
    perm_ref, xcat_ref, at_ref, table_ref, kp_ref, grad_ref, prior_ref,
    edge_ref, hsend_ref, hrecv_ref, halo_ref, mine_ref, theirs_ref, rblk_ref,
    send_sem, recv_sem,
):
    bands = cube_ref.shape[0]
    rows = bands * BLOCK
    h = lax.axis_index("band")
    t = lax.axis_index("tile")
    group = lax.axis_index("groups")
    partner = (group, t, 1 - h)
    left = (group, lax.rem(t + tiles - 1, tiles), h)
    right = (group, lax.rem(t + 1, tiles), h)

    barrier = pltpu.get_barrier_semaphore()
    for device in (partner, left, right):
        pl.semaphore_signal(barrier, inc=1, device_id=device, device_id_type=MESH)

    for pair in range(8):
        two = cube_ref[:, pair * 16 : pair * 16 + 16, :].astype(F32)
        for k in range(2):
            i = pair * 2 + k
            xcat_ref[:, i * 128 : i * 128 + 128] = (
                two[:, k * 8 : k * 8 + 8].reshape(rows, 128).astype(BF16)
            )

    sel_row = iota((2048, 128), 0)
    sel_lane = iota((2048, 128), 1)
    wanted = (sel_lane // 2) * 128 + jnp.where(sel_lane % 2 == 0, 127, 0)
    hsend_ref[...] = dot(xcat_ref[...], onehot(sel_row == wanted)).astype(BF16)

    pl.semaphore_wait(barrier, 3)
    copies = [
        pltpu.make_async_remote_copy(
            src_ref=src, dst_ref=dst, send_sem=send_sem.at[k], recv_sem=recv_sem.at[k],
            device_id=device, device_id_type=MESH,
        )
        for k, (src, dst, device) in enumerate(
            (
                (cube_ref.at[(bands - 1) * (1 - h)], edge_ref, partner),
                (hsend_ref, hrecv_ref.at[0], right),
                (hsend_ref, hrecv_ref.at[1], left),
                (mine_ref, theirs_ref, partner),
            )
        )
    ]
    for copy in copies[:3]:
        copy.start()

    for p in range(8):
        n = iota((128, 1024), 0)
        k = iota((128, 1024), 1)
        perm_ref[p * 128 : p * 128 + 128, :] = onehot(k == (n // 16) * 128 + (n % 16) * 8 + p)

    for half in range(2):
        blocks = dot_nt(perm_ref[...], xcat_ref[:, half * 1024 : half * 1024 + 1024])
        for p in range(8):
            at_ref[half * 128 : half * 128 + 128, p * rows : p * rows + rows] = blocks[
                p * 128 : p * 128 + 128
            ].astype(BF16)

    i = iota((256, 256), 0)
    j = iota((256, 256), 1)
    swap = onehot(j == (i // 64) * 64 + (i % 8) * 8 + (i // 8) % 8)
    kp_ref[:, :, 128:256] = jnp.zeros((kp_ref.shape[0], PIX, 128), F32)
    for g in range(kp_ref.shape[0] // 4):
        four = kern_ref[g * 4 : g * 4 + 4].reshape(256, SUP * PIX)
        kp_ref[g * 4 : g * 4 + 4, :, 0 : SUP * PIX] = dot(swap, four).reshape(4, PIX, SUP * PIX)

    def gather(pair, carry):
        for z in range(ZONES):
            first = kp_ref[kidx_ref[h * bands + pair * 2, z]]
            second = kp_ref[kidx_ref[h * bands + pair * 2 + 1, z]]
            for p in range(8):
                chunk = jnp.concatenate(
                    [first[p * 8 : p * 8 + 8], second[p * 8 : p * 8 + 8]], axis=0
                )
                at = pl.multiple_of(p * rows + pair * 16, 16)
                table_ref[pl.ds(at, 16), z * 256 : z * 256 + 256] = chunk.astype(BF16)
        return carry

    lax.fori_loop(0, bands // 2, gather, 0)

    zone = zone_ref[...].astype(F32).astype(BF16)
    spread_col = dot(onehot(iota((256, 16), 0) // 16 == iota((256, 16), 1)), zone)
    keep = iota((256, 16), 0) % 16 == iota((256, 16), 1)
    zone_col = jnp.sum(jnp.where(keep, spread_col, 0.0), axis=1, keepdims=True)
    spread_row = dot(zone, onehot(iota((16, 256), 1) % 16 == iota((16, 256), 0)))
    keep = iota((16, 256), 1) // 16 == iota((16, 256), 0)
    zone_row = jnp.sum(jnp.where(keep, spread_row, 0.0), axis=0, keepdims=True)

    every = dot(at_ref[...], table_ref[...])
    chosen = jnp.zeros((256, 256), F32)
    for z in range(ZONES):
        chosen = jnp.where(zone_col == float(z), every[:, z * 256 : z * 256 + 256], chosen)
    across = chosen.T
    lane = iota((PIX, 256), 1)
    up = pltpu.roll(across[0:PIX], 240, 1)
    down = pltpu.roll(across[2 * PIX : 3 * PIX], 16, 1)
    partial = (
        across[PIX : 2 * PIX]
        + jnp.where(lane < 240, up, 0.0)
        + jnp.where(lane >= 16, down, 0.0)
    )
    for half in range(2):
        mine_ref[half * PIX : half * PIX + PIX, :] = partial[:, half * 128 : half * 128 + 128]
    copies[3].start()

    for copy in copies[:3]:
        copy.wait()
    even = iota((rows, 128), 1) % 2 == 0
    from_left = jnp.where(t > 0, hrecv_ref[0].astype(F32), 0.0)
    from_right = jnp.where(t < tiles - 1, hrecv_ref[1].astype(F32), 0.0)
    halo_ref[...] = jnp.where(even, from_left, from_right)

    lane = iota((128, 128), 1)
    row = iota((128, 128), 0)

    def prior_of(b, carry):
        x = cube_ref[b].astype(F32)
        edge = edge_ref[...].astype(F32)
        before = cube_ref[jnp.maximum(b - 1, 0)].astype(F32)
        after = cube_ref[jnp.minimum(b + 1, bands - 1)].astype(F32)
        before = jnp.where(b > 0, before, jnp.where(h > 0, edge, 0.0))
        after = jnp.where(b < bands - 1, after, jnp.where(h < 1, edge, 0.0))
        one = halo_ref[pl.ds(pl.multiple_of(b * 8, 8), 8), :]
        rim = jnp.concatenate(
            [pltpu.roll(one, 127 - 2 * i, 1) for i in range(16)], axis=0
        )
        west = pltpu.roll(jnp.where(lane == 127, rim, x), 1, 1)
        east = pltpu.roll(jnp.where(lane == 0, rim, x), 127, 1)
        terms = [
            taps_ref[a, 0] * west + taps_ref[a, 1] * x + taps_ref[a, 2] * east
            for a in range(3)
        ]
        spatial = (
            terms[1]
            + jnp.where(row > 0, pltpu.roll(terms[0], 1, 0), 0.0)
            + jnp.where(row < 127, pltpu.roll(terms[2], 127, 0), 0.0)
        )
        prior_ref[b] = spatial + weight_ref[b] * (2.0 * x - before - after)
        return carry

    lax.fori_loop(0, bands, prior_of, 0)

    copies[3].wait()
    mine_ref[...] = mine_ref[...] + theirs_ref[...]
    flat = jnp.concatenate(
        [
            jnp.concatenate(
                [
                    mine_ref[pl.ds(half * PIX + q, 8, stride=8), :]
                    for q in range(8)
                ],
                axis=1,
            )
            for half in range(2)
        ],
        axis=0,
    )
    high = flat.astype(BF16)
    rest = flat - high.astype(F32)
    mid = rest.astype(BF16)
    low = (rest - mid.astype(F32)).astype(BF16)
    parts = dot(jnp.concatenate([high, mid, low], axis=0), perm_ref[...])
    image = parts[0:16] + (parts[16:32] + parts[32:48])
    residual = []
    for i in range(16):
        half, k = i // 8, i % 8
        piece = (
            image[half * 8 : half * 8 + 8, k * 128 : k * 128 + 128]
            - meas_ref[i * 8 : i * 8 + 8, :]
        )
        res_ref[i * 8 : i * 8 + 8, :] = piece
        residual.append(piece)
    flat = jnp.concatenate(
        [jnp.concatenate(residual[half * 8 : half * 8 + 8], axis=1) for half in range(2)], axis=0
    ).astype(BF16)
    back = dot_nt(flat, perm_ref[...])
    for half in range(2):
        for q in range(8):
            rblk_ref[pl.ds(half * PIX + q, 8, stride=8), :] = back[
                half * 8 : half * 8 + 8, q * 128 : q * 128 + 128
            ]
    centre = jnp.concatenate([rblk_ref[0:PIX, :], rblk_ref[PIX : 2 * PIX, :]], axis=1)
    lane = iota((PIX, 256), 1)
    above = jnp.where(lane >= 16, pltpu.roll(centre, 16, 1), 0.0)
    below = jnp.where(lane < 240, pltpu.roll(centre, 240, 1), 0.0)
    stacked = jnp.concatenate([above, centre, below, jnp.zeros((PIX, 256), F32)], axis=0)
    zoned = jnp.concatenate(
        [jnp.where(zone_row == float(z), stacked, 0.0) for z in range(ZONES)], axis=0
    ).astype(BF16)

    for p in range(8):
        grad_ref[p] = dot(table_ref[p * rows : p * rows + rows, :], zoned)
    for half in range(2):
        wide = jnp.concatenate(
            [grad_ref[p, :, half * 128 : half * 128 + 128] for p in range(8)], axis=1
        )
        high = wide.astype(BF16)
        low = (wide - high.astype(F32)).astype(BF16)
        gradient = dot(high, perm_ref[...]) + dot(low, perm_ref[...])
        for k in range(8):
            i = half * 8 + k
            prior_ref[:, i * 8 : i * 8 + 8, :] = prior_ref[:, i * 8 : i * 8 + 8, :] + gradient[
                :, k * 128 : k * 128 + 128
            ].reshape(bands, 8, 128)

    def update(b, carry):
        out_ref[b] = (cube_ref[b].astype(F32) - step_ref[b] * prior_ref[b]).astype(BF16)
        return carry

    lax.fori_loop(0, bands, update, 0)


def per_device(
    tiles, cube, kernels, zone_map, kernel_index, measurement, step_size, spectral_weight,
    prior_taps,
):
    bands, height, width = cube.shape
    strip = measurement.shape[0]
    rows = bands * BLOCK
    moved = lax.all_to_all(measurement, "tile", split_axis=1, concat_axis=0, tiled=True)
    both = lax.all_gather(moved, "band", axis=0, tiled=False)
    image = both.reshape(2, tiles, strip, width).transpose(1, 0, 2, 3).reshape(height, width)
    vmem = pl.BlockSpec(memory_space=pltpu.VMEM)
    smem = pl.BlockSpec(memory_space=pltpu.SMEM)
    updated, residual = pl.pallas_call(
        functools.partial(kernel, tiles),
        out_shape=(
            jax.ShapeDtypeStruct(cube.shape, BF16),
            jax.ShapeDtypeStruct((height, width), F32),
        ),
        in_specs=[vmem] * 4 + [smem] * 4,
        out_specs=(vmem, vmem),
        scratch_shapes=[
            pltpu.VMEM((1024, 1024), BF16),
            pltpu.VMEM((rows, 2048), BF16),
            pltpu.VMEM((256, 8 * rows), BF16),
            pltpu.VMEM((8 * rows, ZONES * 256), BF16),
            pltpu.VMEM((kernels.shape[0], PIX, 256), F32),
            pltpu.VMEM((8, rows, 256), F32),
            pltpu.VMEM(cube.shape, F32),
            pltpu.VMEM((height, width), BF16),
            pltpu.VMEM((rows, 128), BF16),
            pltpu.VMEM((2, rows, 128), BF16),
            pltpu.VMEM((rows, 128), F32),
            pltpu.VMEM((2 * PIX, 128), F32),
            pltpu.VMEM((2 * PIX, 128), F32),
            pltpu.VMEM((2 * PIX, 128), F32),
            pltpu.SemaphoreType.DMA((4,)),
            pltpu.SemaphoreType.DMA((4,)),
        ],
        compiler_params=pltpu.CompilerParams(
            collective_id=0, has_side_effects=True, vmem_limit_bytes=50 << 20
        ),
    )(cube, kernels, zone_map, image, kernel_index, step_size, spectral_weight, prior_taps)
    own = lax.dynamic_index_in_dim(
        residual.reshape(tiles, 2, strip, width), lax.axis_index("band"), 1, keepdims=False
    ).reshape(tiles * strip, width)
    return updated, lax.all_to_all(own, "tile", split_axis=0, concat_axis=1, tiled=True)


def solution(mesh):
    return jax.shard_map(
        functools.partial(per_device, mesh.shape["tile"]),
        mesh=mesh,
        in_specs=(
            P(("groups", "band"), None, "tile"),
            P(),
            P(None, "tile"),
            P(),
            P(("groups", "tile", "band"), None),
            P("band"),
            P("band"),
            P(),
        ),
        out_specs=(P(("groups", "band"), None, "tile"), P(("groups", "tile", "band"), None)),
        check_vma=False,
    )
```

profile of v0, /device:TPU:0, one launch (start us, length us, event | category | flops | bytes accessed | tf_op | source)
XLA Modules:
  0.0 50.8 jit_solution(15692114085370413752)
XLA Ops:
  0.6 7.3 %all-to-all-start = ((f32[8,8,128]{2,0,1:T(8,128)}), f32[8,8,128]{2,0,1:T(8,128)S(1)}, u32[]{:S(2)}, u32[]{:S(2)}) async-start(f32[8,8,128]{2,0,1:T(8,128)} %bitcast.19), calls=%async_computation | async-start | bytes 65536 | tf_op jit(solution)/shard_map/all_to_all | solution.py:261
  7.9 0.0 copy-start.6
  7.9 0.7 %copy-done.6 = s32[64,4]{0,1:T(4,128)S(1)} copy-done((s32[64,4]{0,1:T(4,128)S(1)}, s32[64,4]{0,1:T(4,128)}, u32[]{:S(2)}) %copy-start.6) | copy-done | bytes 1048
  8.6 0.1 copy.14.kidx_ref
  8.7 5.9 %all-to-all-done = f32[8,8,128]{2,0,1:T(8,128)S(1)} async-done(((f32[8,8,128]{2,0,1:T(8,128)}), f32[8,8,128]{2,0,1:T(8,128)S(1)}, u32[]{:S(2)}, u32[]{:S(2)}) %all-to-all-start) | async-done | bytes 32800 | tf_op jit(solution)/shard_map/all_to_all | solution.py:261
  14.6 1.8 %all_gather.7 = f32[2,64,128]{2,1,0:T(8,128)S(1)} all-gather(f32[1,64,128]{2,1,0:T(8,128)S(1)} %bitcast.17), channel_id=1, replica_groups=mesh['groups'=2,'tile'=8,'band'=2] {'band'}, dimensions={0}, use_global_device_ids=true | all-gather | bytes 98304 | tf_op jit(solution)/shard_map/all_gather | solution.py:262
  16.4 0.0 copy-start.2
  16.4 0.0 copy-start.3
  16.4 0.0 copy-start.4
  16.4 0.0 copy-start.5
  16.5 0.7 %copy-done.2 = s32[16,16]{1,0:T(8,128)S(1)} copy-done((s32[16,16]{1,0:T(8,128)S(1)}, s32[16,16]{1,0:T(8,128)}, u32[]{:S(2)}) %copy-start.2) | copy-done | bytes 1048
  17.1 0.0 copy-done.3
  17.1 0.0 copy-done.4
  17.1 0.0 copy-done.5
  17.1 0.0 copy-start
  17.1 1.2 %copy-done = bf16[32,128,128]{2,1,0:T(8,128)(2,1)S(1)} copy-done((bf16[32,128,128]{2,1,0:T(8,128)(2,1)S(1)}, bf16[32,128,128]{2,1,0:T(8,128)(2,1)}, u32[]{:S(2)}) %copy-start) | copy-done | bytes 1048600
  18.4 0.0 copy-start.1
  18.4 1.2 %copy-done.1 = bf16[32,64,192]{2,1,0:T(8,128)(2,1)S(1)} copy-done((bf16[32,64,192]{2,1,0:T(8,128)(2,1)S(1)}, bf16[32,64,192]{2,1,0:T(8,128)(2,1)}, u32[]{:S(2)}) %copy-start.1) | copy-done | bytes 786456
  19.6 19.0 %shard_map.95 = (bf16[32,128,128]{2,1,0:T(8,128)(2,1)S(1)}, f32[128,128]{1,0:T(8,128)S(1)}) custom-call(bf16[32,128,128]{2,1,0:T(8,128)(2,1)S(1)} %copy-done, bf16[32,64,192]{2,1,0:T(8,128)(2,1)S(1)} %copy-done.1, s32[16,16]{1,0:T(8,128)S(1)} %copy-done.2, f32[128,128]{1,0:T(8,128)S(1)} %bitcast.14, s32[64,4]{1,0:T(8,128)S(1)} %copy.14.kidx_ref, ...), custom_call_target="tpu_custom_call" | custom-call | tf_op jit(solution)/shard_map/pallas_call | solution.py:266
  38.6 0.6 %dynamic-slice_bitcast_fusion = f32[8,8,128]{2,1,0:T(8,128)} fusion(f32[8,2,8,128]{3,2,1,0:T(8,128)S(1)} %bitcast.15, s32[]{:T(128)S(6)} %select_n.4), kind=kLoop, calls=%fused_computation | loop fusion | bytes 65540 | tf_op jit(solution)/shard_map/all_to_all | solution.py:299
  39.3 3.3 %all-to-all-start.1 = ((f32[8,8,128]{2,1,0:T(8,128)}), f32[8,8,128]{2,1,0:T(8,128)S(1)}, u32[]{:S(2)}, u32[]{:S(2)}) async-start(f32[8,8,128]{2,1,0:T(8,128)} %dynamic-slice_bitcast_fusion), calls=%async_computation.1 | async-start | bytes 65536 | tf_op jit(solution)/shard_map/all_to_all | solution.py:299
  42.6 6.6 %all-to-all-done.1 = f32[8,8,128]{2,1,0:T(8,128)S(1)} async-done(((f32[8,8,128]{2,1,0:T(8,128)}), f32[8,8,128]{2,1,0:T(8,128)S(1)}, u32[]{:S(2)}, u32[]{:S(2)}) %all-to-all-start.1) | async-done | bytes 32800 | tf_op jit(solution)/shard_map/all_to_all | solution.py:299
  49.2 1.0 %copy.17 = bf16[32,128,128]{2,1,0:T(8,128)(2,1)} copy(bf16[32,128,128]{2,1,0:T(8,128)(2,1)S(1)} %get-tuple-element.8) | data formatting | bytes 2097152
  50.2 0.6 %copy.18 = f32[8,1024]{1,0:T(8,128)} copy(f32[8,1024]{1,0:T(8,128)S(1)} %bitcast.18) | data formatting | bytes 65536
  (1 shorter events, 0.0 us)
Async XLA Ops:
  0.6 14.0 %all-to-all-start = ((f32[8,8,128]{2,0,1:T(8,128)}), f32[8,8,128]{2,0,1:T(8,128)S(1)}, u32[]{:S(2)}, u32[]{:S(2)}) async-start(f32[8,8,128]{2,0,1:T(8,128)} %bitcast.19), calls=%async_computation | async-start | bytes 65536 | tf_op jit(solution)/shard_map/all_to_all | solution.py:261
  7.9 0.7 %copy-start.6 = (s32[64,4]{0,1:T(4,128)S(1)}, s32[64,4]{0,1:T(4,128)}, u32[]{:S(2)}) copy-start(s32[64,4]{0,1:T(4,128)} %param.11) | copy-start | bytes 3076
  16.4 0.7 %copy-start.2 = (s32[16,16]{1,0:T(8,128)S(1)}, s32[16,16]{1,0:T(8,128)}, u32[]{:S(2)}) copy-start(s32[16,16]{1,0:T(8,128)} %zone_ref.1) | copy-start | bytes 3076
  16.4 0.7 %copy-start.3 = (f32[3,3]{1,0:T(4,128)S(1)}, f32[3,3]{1,0:T(4,128)}, u32[]{:S(2)}) copy-start(f32[3,3]{1,0:T(4,128)} %taps_ref.1) | copy-start | bytes 112
  16.4 0.7 %copy-start.4 = (f32[32]{0:T(128)S(1)}, f32[32]{0:T(128)}, u32[]{:S(2)}) copy-start(f32[32]{0:T(128)} %step_ref.1) | copy-start | bytes 388
  16.4 0.7 %copy-start.5 = (f32[32]{0:T(128)S(1)}, f32[32]{0:T(128)}, u32[]{:S(2)}) copy-start(f32[32]{0:T(128)} %weight_ref.1) | copy-start | bytes 388
  17.1 1.2 %copy-start = (bf16[32,128,128]{2,1,0:T(8,128)(2,1)S(1)}, bf16[32,128,128]{2,1,0:T(8,128)(2,1)}, u32[]{:S(2)}) copy-start(bf16[32,128,128]{2,1,0:T(8,128)(2,1)} %cube_ref.1) | copy-start | bytes 3145732
  18.4 1.2 %copy-start.1 = (bf16[32,64,192]{2,1,0:T(8,128)(2,1)S(1)}, bf16[32,64,192]{2,1,0:T(8,128)(2,1)}, u32[]{:S(2)}) copy-start(bf16[32,64,192]{2,1,0:T(8,128)(2,1)} %kern_ref.1) | copy-start | bytes 2359300
  39.3 10.0 %all-to-all-start.1 = ((f32[8,8,128]{2,1,0:T(8,128)}), f32[8,8,128]{2,1,0:T(8,128)S(1)}, u32[]{:S(2)}, u32[]{:S(2)}) async-start(f32[8,8,128]{2,1,0:T(8,128)} %dynamic-slice_bitcast_fusion), calls=%async_computation.1 | async-start | bytes 65536 | tf_op jit(solution)/shard_map/all_to_all | solution.py:299
where the time goes:
time: 51.2 us; the launch traced here: 50.8 us
  Pallas kernels  19 us (37%)
  waiting for transfers between devices  12.5 us (24%)
  starting transfers between devices  10.6 us (21%)
  local copies, waits for them, and re-layouts  6.11 us (12%)
  blocking collectives  1.84 us (4%)
  between operations  0.68 us (1%)
    pallas_call x1, Pallas kernels, per_device(): pl.pallas_call(functools.partial(kernel, tiles), out_shape=(jax.ShapeDtyp...  19 us
    all_to_all x1, starting transfers between devices, per_device(): lax.all_to_all(measurement, 'tile', split_axis=1, concat_axis=0, tiled=True)  7.26 us
    all_to_all x1, waiting for transfers between devices, per_device(): lax.all_to_all(own, 'tile', split_axis=0, concat_axis=1, tiled=True)  6.62 us
    all_to_all x1, waiting for transfers between devices, per_device(): lax.all_to_all(measurement, 'tile', split_axis=1, concat_axis=0, tiled=True)  5.91 us
    unnamed x17, local copies, waits for them, and re-layouts  5.48 us
    all_to_all x1, starting transfers between devices, per_device(): lax.all_to_all(own, 'tile', split_axis=0, concat_axis=1, tiled=True)  3.34 us
    all_gather x1, blocking collectives, per_device(): both = lax.all_gather(moved, 'band', axis=0, tiled=False)  1.84 us
  transfers between devices with their start and end apart: 2, of which 2 were waited for; matrix products, arithmetic and copies ran while one was open for 0% of the time, Pallas kernels for 0%

commit v1 on v0

--- a/solution.py
+++ b/solution.py
@@ -34,12 +34,12 @@
 
 
 def kernel(
-    tiles,
-    cube_ref, kern_ref, zone_ref, meas_ref, kidx_ref, step_ref, weight_ref, taps_ref,
+    tiles, direct,
+    cube_hbm, kern_hbm, zone_ref, meas_ref, kidx_ref, step_ref, weight_ref, taps_ref,
     out_ref, res_ref,
-    perm_ref, xcat_ref, at_ref, table_ref, kp_ref, grad_ref, prior_ref,
+    cube_ref, kern_ref, meas_blocks, res_blocks, perm_ref, xcat_ref, at_ref, table_ref, kp_ref, grad_ref, prior_ref,
     edge_ref, hsend_ref, hrecv_ref, halo_ref, mine_ref, theirs_ref, rblk_ref,
-    send_sem, recv_sem,
+    load_sem, send_sem, recv_sem,
 ):
     bands = cube_ref.shape[0]
     rows = bands * BLOCK
@@ -50,10 +50,64 @@
     left = (group, lax.rem(t + tiles - 1, tiles), h)
     right = (group, lax.rem(t + 1, tiles), h)
 
+    load_cube = pltpu.make_async_copy(cube_hbm, cube_ref, load_sem.at[0])
+    load_kern = pltpu.make_async_copy(kern_hbm, kern_ref, load_sem.at[1])
+    load_cube.start()
+    load_kern.start()
+
+    me = 2 * t + h
+    count = 2 * tiles
+    others = []
+    if direct:
+        for d in range(1, count):
+            peer = lax.rem(me + d, count)
+            others.append((peer // 2, (group, peer // 2, lax.rem(peer, 2))))
+        greeted = [device for _, device in others]
+    else:
+        greeted = [partner, left, right]
     barrier = pltpu.get_barrier_semaphore()
-    for device in (partner, left, right):
+    for device in greeted:
         pl.semaphore_signal(barrier, inc=1, device_id=device, device_id_type=MESH)
 
+    for p in range(8):
+        n = iota((128, 1024), 0)
+        k = iota((128, 1024), 1)
+        perm_ref[p * 128 : p * 128 + 128, :] = onehot(k == (n // 16) * 128 + (n % 16) * 8 + p)
+
+    def remote(k, src, dst, device):
+        return pltpu.make_async_remote_copy(
+            src_ref=src, dst_ref=dst, send_sem=send_sem.at[k], recv_sem=recv_sem.at[k],
+            device_id=device, device_id_type=MESH,
+        )
+
+    pl.semaphore_wait(barrier, len(greeted))
+    copies = [
+        remote(0, cube_hbm.at[(bands - 1) * (1 - h)], edge_ref, partner),
+        remote(1, hsend_ref, hrecv_ref.at[0], right),
+        remote(2, hsend_ref, hrecv_ref.at[1], left),
+        remote(3, mine_ref, theirs_ref, partner),
+    ]
+    copies[0].start()
+    meas_copies = [
+        remote(
+            3 + d,
+            meas_ref.at[:, pl.ds(pl.multiple_of(tile * 128, 128), 128)],
+            meas_blocks.at[me],
+            device,
+        )
+        for d, (tile, device) in enumerate(others, 1)
+    ]
+    for copy in meas_copies:
+        copy.start()
+    if direct:
+        load_own = pltpu.make_async_copy(
+            meas_ref.at[:, pl.ds(pl.multiple_of(t * 128, 128), 128)],
+            meas_blocks.at[me],
+            load_sem.at[2],
+        )
+        load_own.start()
+
+    load_cube.wait()
     for pair in range(8):
         two = cube_ref[:, pair * 16 : pair * 16 + 16, :].astype(F32)
         for k in range(2):
@@ -67,28 +121,8 @@
     wanted = (sel_lane // 2) * 128 + jnp.where(sel_lane % 2 == 0, 127, 0)
     hsend_ref[...] = dot(xcat_ref[...], onehot(sel_row == wanted)).astype(BF16)
 
-    pl.semaphore_wait(barrier, 3)
-    copies = [
-        pltpu.make_async_remote_copy(
-            src_ref=src, dst_ref=dst, send_sem=send_sem.at[k], recv_sem=recv_sem.at[k],
-            device_id=device, device_id_type=MESH,
-        )
-        for k, (src, dst, device) in enumerate(
-            (
-                (cube_ref.at[(bands - 1) * (1 - h)], edge_ref, partner),
-                (hsend_ref, hrecv_ref.at[0], right),
-                (hsend_ref, hrecv_ref.at[1], left),
-                (mine_ref, theirs_ref, partner),
-            )
-        )
-    ]
-    for copy in copies[:3]:
-        copy.start()
-
-    for p in range(8):
-        n = iota((128, 1024), 0)
-        k = iota((128, 1024), 1)
-        perm_ref[p * 128 : p * 128 + 128, :] = onehot(k == (n // 16) * 128 + (n % 16) * 8 + p)
+    copies[1].start()
+    copies[2].start()
 
     for half in range(2):
         blocks = dot_nt(perm_ref[...], xcat_ref[:, half * 1024 : half * 1024 + 1024])
@@ -97,6 +131,7 @@
                 p * 128 : p * 128 + 128
             ].astype(BF16)
 
+    load_kern.wait()
     i = iota((256, 256), 0)
     j = iota((256, 256), 1)
     swap = onehot(j == (i // 64) * 64 + (i % 8) * 8 + (i // 8) % 8)
@@ -107,8 +142,8 @@
 
     def gather(pair, carry):
         for z in range(ZONES):
-            first = kp_ref[kidx_ref[h * bands + pair * 2, z]]
-            second = kp_ref[kidx_ref[h * bands + pair * 2 + 1, z]]
+            first = kp_ref[kidx_ref[z, h * bands + pair * 2]]
+            second = kp_ref[kidx_ref[z, h * bands + pair * 2 + 1]]
             for p in range(8):
                 chunk = jnp.concatenate(
                     [first[p * 8 : p * 8 + 8], second[p * 8 : p * 8 + 8]], axis=0
@@ -202,15 +237,34 @@
     low = (rest - mid.astype(F32)).astype(BF16)
     parts = dot(jnp.concatenate([high, mid, low], axis=0), perm_ref[...])
     image = parts[0:16] + (parts[16:32] + parts[32:48])
+    if direct:
+        load_own.wait()
+        for copy in meas_copies:
+            copy.wait()
     residual = []
     for i in range(16):
         half, k = i // 8, i % 8
-        piece = (
-            image[half * 8 : half * 8 + 8, k * 128 : k * 128 + 128]
-            - meas_ref[i * 8 : i * 8 + 8, :]
-        )
-        res_ref[i * 8 : i * 8 + 8, :] = piece
+        piece = image[half * 8 : half * 8 + 8, k * 128 : k * 128 + 128]
+        if direct:
+            piece = piece - meas_blocks[i]
+            res_blocks[i] = piece
+        else:
+            piece = piece - meas_ref[i * 8 : i * 8 + 8, :]
+            res_ref[i * 8 : i * 8 + 8, :] = piece
         residual.append(piece)
+    res_copies = []
+    if direct:
+        own = pl.ds(pl.multiple_of(t * 128, 128), 128)
+        for d in range(1, tiles):
+            tile = lax.rem(t + d, tiles)
+            res_copies.append(
+                remote(
+                    2 + count + d, res_blocks.at[2 * tile + h], res_ref.at[:, own], (group, tile, h)
+                )
+            )
+        for copy in res_copies:
+            copy.start()
+        res_ref[:, own] = res_blocks[me]
     flat = jnp.concatenate(
         [jnp.concatenate(residual[half * 8 : half * 8 + 8], axis=1) for half in range(2)], axis=0
     ).astype(BF16)
@@ -249,6 +303,8 @@
         return carry
 
     lax.fori_loop(0, bands, update, 0)
+    for copy in res_copies:
+        copy.wait()
 
 
 def per_device(
@@ -258,20 +314,31 @@
     bands, height, width = cube.shape
     strip = measurement.shape[0]
     rows = bands * BLOCK
-    moved = lax.all_to_all(measurement, "tile", split_axis=1, concat_axis=0, tiled=True)
-    both = lax.all_gather(moved, "band", axis=0, tiled=False)
-    image = both.reshape(2, tiles, strip, width).transpose(1, 0, 2, 3).reshape(height, width)
+    direct = strip == BLOCK and width == 128
+    if direct:
+        image = measurement
+        sems = 3 + 2 * tiles + tiles
+    else:
+        moved = lax.all_to_all(measurement, "tile", split_axis=1, concat_axis=0, tiled=True)
+        both = lax.all_gather(moved, "band", axis=0, tiled=False)
+        image = both.reshape(2, tiles, strip, width).transpose(1, 0, 2, 3).reshape(height, width)
+        sems = 4
+    hbm = pl.BlockSpec(memory_space=pltpu.HBM)
     vmem = pl.BlockSpec(memory_space=pltpu.VMEM)
     smem = pl.BlockSpec(memory_space=pltpu.SMEM)
     updated, residual = pl.pallas_call(
-        functools.partial(kernel, tiles),
+        functools.partial(kernel, tiles, direct),
         out_shape=(
             jax.ShapeDtypeStruct(cube.shape, BF16),
-            jax.ShapeDtypeStruct((height, width), F32),
+            jax.ShapeDtypeStruct(image.shape, F32),
         ),
-        in_specs=[vmem] * 4 + [smem] * 4,
+        in_specs=[hbm, hbm, vmem, hbm if direct else vmem] + [smem] * 4,
         out_specs=(vmem, vmem),
         scratch_shapes=[
+            pltpu.VMEM(cube.shape, BF16),
+            pltpu.VMEM(kernels.shape, BF16),
+            pltpu.VMEM((height // BLOCK, BLOCK, width), F32),
+            pltpu.VMEM((height // BLOCK, BLOCK, width), F32),
             pltpu.VMEM((1024, 1024), BF16),
             pltpu.VMEM((rows, 2048), BF16),
             pltpu.VMEM((256, 8 * rows), BF16),
@@ -286,13 +353,16 @@
             pltpu.VMEM((2 * PIX, 128), F32),
             pltpu.VMEM((2 * PIX, 128), F32),
             pltpu.VMEM((2 * PIX, 128), F32),
-            pltpu.SemaphoreType.DMA((4,)),
-            pltpu.SemaphoreType.DMA((4,)),
+            pltpu.SemaphoreType.DMA((3,)),
+            pltpu.SemaphoreType.DMA((sems,)),
+            pltpu.SemaphoreType.DMA((sems,)),
         ],
         compiler_params=pltpu.CompilerParams(
             collective_id=0, has_side_effects=True, vmem_limit_bytes=50 << 20
         ),
-    )(cube, kernels, zone_map, image, kernel_index, step_size, spectral_weight, prior_taps)
+    )(cube, kernels, zone_map, image, kernel_index.T, step_size, spectral_weight, prior_taps)
+    if direct:
+        return updated, residual
     own = lax.dynamic_index_in_dim(
         residual.reshape(tiles, 2, strip, width), lax.axis_index("band"), 1, keepdims=False
     ).reshape(tiles * strip, width)

time: 51.2 us -> 32.2 us (0.63)
  waiting for transfers between devices: 12.5 us -> 0 us
  starting transfers between devices: 10.6 us -> 0 us
  Pallas kernels: 19 us -> 23.7 us
  blocking collectives: 1.84 us -> 0 us
  local copies, waits for them, and re-layouts: 6.11 us -> 7.51 us
    all_to_all x2 -> x0, waiting for transfers between devices: 12.5 us -> none  [the longest x1 6.62 us: per_device(): lax.all_to_all(own, 'tile', split_axis=0, concat_axis=1, tiled=True)]
    all_to_all x2 -> x0, starting transfers between devices: 10.6 us -> none  [the longest x1 7.26 us: per_device(): lax.all_to_all(measurement, 'tile', split_axis=1, concat_axis=0, tiled=True)]
    pallas_call x1, Pallas kernels: 19 us -> 23.7 us  [per_device(): pl.pallas_call(functools.partial(kernel, tiles, direct), out_shape=(jax.S...]
    unnamed x17 -> x18, local copies, waits for them, and re-layouts: 5.48 us -> 7.51 us
    all_gather x1 -> x0, blocking collectives: 1.84 us -> none  [per_device(): both = lax.all_gather(moved, 'band', axis=0, tiled=False)]
    all_to_all x1 -> x0, local copies, waits for them, and re-layouts: 0.63 us -> none  [per_device(): lax.all_to_all(own, 'tile', split_axis=0, concat_axis=1, tiled=True)]
  transfers between devices with their start and end apart: 2 -> 0, of which waited for: 2 -> 0; matrix products, arithmetic and copies ran while one was open for 0% -> 0% of each run, Pallas kernels for 0% -> 0%
where the time goes in v1:
time: 32.2 us; the launch traced here: 31.8 us
  Pallas kernels  23.7 us (74%)
  local copies, waits for them, and re-layouts  7.51 us (23%)
  between operations  0.66 us (2%)
    pallas_call x1, Pallas kernels, per_device(): pl.pallas_call(functools.partial(kernel, tiles, direct), out_shape=(jax.S...  23.7 us
    unnamed x18, local copies, waits for them, and re-layouts  7.51 us

profile of v1, /device:TPU:0, one launch (start us, length us, event | category | flops | bytes accessed | tf_op | source)
XLA Modules:
  0.0 31.8 jit_solution(15181474572891902393)
XLA Ops:
  0.6 0.0 copy-start.7
  0.6 0.0 copy-start.6
  0.7 0.6 %copy-done.7 = f32[32]{0:T(128)S(1)} copy-done((f32[32]{0:T(128)S(1)}, f32[32]{0:T(128)}, u32[]{:S(2)}) %copy-start.7) | copy-done | bytes 152
  1.3 0.0 copy-done.6
  1.3 0.0 copy-start
  1.3 1.2 %copy-done = bf16[32,128,128]{2,1,0:T(8,128)(2,1)S(1)} copy-done((bf16[32,128,128]{2,1,0:T(8,128)(2,1)S(1)}, bf16[32,128,128]{2,1,0:T(8,128)(2,1)}, u32[]{:S(2)}) %copy-start) | copy-done | bytes 1048600
  2.5 0.0 copy-start.1
  2.5 1.2 %copy-done.1 = bf16[32,64,192]{2,1,0:T(8,128)(2,1)S(1)} copy-done((bf16[32,64,192]{2,1,0:T(8,128)(2,1)S(1)}, bf16[32,64,192]{2,1,0:T(8,128)(2,1)}, u32[]{:S(2)}) %copy-start.1) | copy-done | bytes 786456
  3.8 0.0 copy-start.2
  3.8 0.8 %copy-done.2 = f32[8,1024]{1,0:T(8,128)S(1)} copy-done((f32[8,1024]{1,0:T(8,128)S(1)}, f32[8,1024]{1,0:T(8,128)}, u32[]{:S(2)}) %copy-start.2) | copy-done | bytes 32792
  4.5 0.0 copy-start.3
  4.5 0.7 %copy-done.3 = s32[16,16]{1,0:T(8,128)S(1)} copy-done((s32[16,16]{1,0:T(8,128)S(1)}, s32[16,16]{1,0:T(8,128)}, u32[]{:S(2)}) %copy-start.3) | copy-done | bytes 1048
  5.2 0.0 copy-start.4
  5.2 0.7 %copy-done.4 = s32[64,4]{0,1:T(4,128)S(1)} copy-done((s32[64,4]{0,1:T(4,128)S(1)}, s32[64,4]{0,1:T(4,128)}, u32[]{:S(2)}) %copy-start.4) | copy-done | bytes 1048
  5.9 0.0 copy-start.5
  5.9 0.7 %copy-done.5 = f32[3,3]{1,0:T(4,128)S(1)} copy-done((f32[3,3]{1,0:T(4,128)S(1)}, f32[3,3]{1,0:T(4,128)}, u32[]{:S(2)}) %copy-start.5) | copy-done | bytes 60
  6.6 23.7 %shard_map.95 = (bf16[32,128,128]{2,1,0:T(8,128)(2,1)S(1)}, f32[8,1024]{1,0:T(8,128)S(1)}) custom-call(bf16[32,128,128]{2,1,0:T(8,128)(2,1)S(1)} %copy-done, bf16[32,64,192]{2,1,0:T(8,128)(2,1)S(1)} %copy-done.1, s32[16,16]{1,0:T(8,128)S(1)} %copy-done.3, f32[8,1024]{1,0:T(8,128)S(1)} %copy-done.2, s32[4,64]{1,0:T(4,128)S(1)} %bitcast.1, f32[32]{0:T(128)S(1)} %copy-done.6, ...), custom_call_target="tpu_custom_call" | custom-call | tf_op jit(solution)/shard_map/pallas_call | solution.py:329
  30.2 1.0 %copy.12 = bf16[32,128,128]{2,1,0:T(8,128)(2,1)} copy(bf16[32,128,128]{2,1,0:T(8,128)(2,1)S(1)} %get-tuple-element.4) | data formatting | bytes 2097152
  31.2 0.6 %copy.13 = f32[8,1024]{1,0:T(8,128)} copy(f32[8,1024]{1,0:T(8,128)S(1)} %get-tuple-element.5) | data formatting | bytes 65536
Async XLA Ops:
  0.6 0.7 %copy-start.7 = (f32[32]{0:T(128)S(1)}, f32[32]{0:T(128)}, u32[]{:S(2)}) copy-start(f32[32]{0:T(128)} %weight_ref.1) | copy-start | bytes 388
  0.6 0.7 %copy-start.6 = (f32[32]{0:T(128)S(1)}, f32[32]{0:T(128)}, u32[]{:S(2)}) copy-start(f32[32]{0:T(128)} %step_ref.1) | copy-start | bytes 388
  1.3 1.2 %copy-start = (bf16[32,128,128]{2,1,0:T(8,128)(2,1)S(1)}, bf16[32,128,128]{2,1,0:T(8,128)(2,1)}, u32[]{:S(2)}) copy-start(bf16[32,128,128]{2,1,0:T(8,128)(2,1)} %cube_hbm.1) | copy-start | bytes 3145732
  2.5 1.2 %copy-start.1 = (bf16[32,64,192]{2,1,0:T(8,128)(2,1)S(1)}, bf16[32,64,192]{2,1,0:T(8,128)(2,1)}, u32[]{:S(2)}) copy-start(bf16[32,64,192]{2,1,0:T(8,128)(2,1)} %kern_hbm.1) | copy-start | bytes 2359300
  3.8 0.8 %copy-start.2 = (f32[8,1024]{1,0:T(8,128)S(1)}, f32[8,1024]{1,0:T(8,128)}, u32[]{:S(2)}) copy-start(f32[8,1024]{1,0:T(8,128)} %meas_ref.1) | copy-start | bytes 98308
  4.5 0.7 %copy-start.3 = (s32[16,16]{1,0:T(8,128)S(1)}, s32[16,16]{1,0:T(8,128)}, u32[]{:S(2)}) copy-start(s32[16,16]{1,0:T(8,128)} %zone_ref.1) | copy-start | bytes 3076
  5.2 0.7 %copy-start.4 = (s32[64,4]{0,1:T(4,128)S(1)}, s32[64,4]{0,1:T(4,128)}, u32[]{:S(2)}) copy-start(s32[64,4]{0,1:T(4,128)} %param.11) | copy-start | bytes 3076
  5.9 0.7 %copy-start.5 = (f32[3,3]{1,0:T(4,128)S(1)}, f32[3,3]{1,0:T(4,128)}, u32[]{:S(2)}) copy-start(f32[3,3]{1,0:T(4,128)} %taps_ref.1) | copy-start | bytes 112

commit v2 on v1

--- a/solution.py
+++ b/solution.py
@@ -36,8 +36,8 @@
 def kernel(
     tiles, direct,
     cube_hbm, kern_hbm, zone_ref, meas_ref, kidx_ref, step_ref, weight_ref, taps_ref,
-    out_ref, res_ref,
-    cube_ref, kern_ref, meas_blocks, res_blocks, perm_ref, xcat_ref, at_ref, table_ref, kp_ref, grad_ref, prior_ref,
+    out_hbm, res_ref,
+    cube_ref, new_ref, grows_ref, rowtaps_ref, along_ref, kern_ref, meas_blocks, res_blocks, perm_ref, xcat_ref, at_ref, table_ref, kp_ref, grad_ref, prior_ref,
     edge_ref, hsend_ref, hrecv_ref, halo_ref, mine_ref, theirs_ref, rblk_ref,
     load_sem, send_sem, recv_sem,
 ):
@@ -186,35 +186,52 @@
     from_right = jnp.where(t < tiles - 1, hrecv_ref[1].astype(F32), 0.0)
     halo_ref[...] = jnp.where(even, from_left, from_right)
 
-    lane = iota((128, 128), 1)
+    source = iota((128, 128), 0)
+    target = iota((128, 128), 1)
+    for a in range(3):
+        first, centre, last = taps_ref[a, 0], taps_ref[a, 1], taps_ref[a, 2]
+        inner = (
+            jnp.where(source == target - 1, first, 0.0)
+            + jnp.where(source == target, centre, 0.0)
+            + jnp.where(source == target + 1, last, 0.0)
+        )
+        outer = jnp.where((target == 0) & (source % 2 == 0), first, 0.0) + jnp.where(
+            (target == 127) & (source % 2 == 1), last, 0.0
+        )
+        taps = jnp.concatenate([inner, outer], axis=0)
+        high = taps.astype(BF16)
+        low = (taps - high.astype(F32)).astype(BF16)
+        rowtaps_ref[0:256, a * 128 : a * 128 + 128] = high
+        rowtaps_ref[256:512, a * 128 : a * 128 + 128] = low
+
     row = iota((128, 128), 0)
-
-    def prior_of(b, carry):
-        x = cube_ref[b].astype(F32)
-        edge = edge_ref[...].astype(F32)
-        before = cube_ref[jnp.maximum(b - 1, 0)].astype(F32)
-        after = cube_ref[jnp.minimum(b + 1, bands - 1)].astype(F32)
-        before = jnp.where(b > 0, before, jnp.where(h > 0, edge, 0.0))
-        after = jnp.where(b < bands - 1, after, jnp.where(h < 1, edge, 0.0))
-        one = halo_ref[pl.ds(pl.multiple_of(b * 8, 8), 8), :]
-        rim = jnp.concatenate(
-            [pltpu.roll(one, 127 - 2 * i, 1) for i in range(16)], axis=0
-        )
-        west = pltpu.roll(jnp.where(lane == 127, rim, x), 1, 1)
-        east = pltpu.roll(jnp.where(lane == 0, rim, x), 127, 1)
-        terms = [
-            taps_ref[a, 0] * west + taps_ref[a, 1] * x + taps_ref[a, 2] * east
-            for a in range(3)
-        ]
-        spatial = (
-            terms[1]
-            + jnp.where(row > 0, pltpu.roll(terms[0], 1, 0), 0.0)
-            + jnp.where(row < 127, pltpu.roll(terms[2], 127, 0), 0.0)
-        )
-        prior_ref[b] = spatial + weight_ref[b] * (2.0 * x - before - after)
-        return carry
-
-    lax.fori_loop(0, bands, prior_of, 0)
+    edge = edge_ref[...].astype(F32)
+    owner = iota((16, 8, 128), 2) // 2 == iota((16, 8, 128), 0)
+    for g in range(bands // 8):
+        inside = cube_ref[g * 8 : g * 8 + 8].reshape(1024, 128)
+        rim = halo_ref[g * 64 : g * 64 + 64, :].reshape(8, 1, 8, 128)
+        rim = jnp.where(owner[None], rim, 0.0).reshape(1024, 128).astype(BF16)
+        along_ref[...] = dot(
+            jnp.concatenate([inside, rim, inside, rim], axis=1), rowtaps_ref[...]
+        )
+        for k in range(8):
+            b = g * 8 + k
+            x = cube_ref[b].astype(F32)
+            if b > 0:
+                before = cube_ref[b - 1].astype(F32)
+            else:
+                before = jnp.where(h > 0, edge, 0.0)
+            if b < bands - 1:
+                after = cube_ref[b + 1].astype(F32)
+            else:
+                after = jnp.where(h < 1, edge, 0.0)
+            span = slice(k * 128, k * 128 + 128)
+            spatial = (
+                along_ref[span, 128:256]
+                + jnp.where(row > 0, pltpu.roll(along_ref[span, 0:128], 1, 0), 0.0)
+                + jnp.where(row < 127, pltpu.roll(along_ref[span, 256:384], 127, 0), 0.0)
+            )
+            prior_ref[b] = spatial + weight_ref[b] * (2.0 * x - before - after)
 
     copies[3].wait()
     mine_ref[...] = mine_ref[...] + theirs_ref[...]
@@ -285,24 +302,33 @@
 
     for p in range(8):
         grad_ref[p] = dot(table_ref[p * rows : p * rows + rows, :], zoned)
+    stores = []
     for half in range(2):
         wide = jnp.concatenate(
             [grad_ref[p, :, half * 128 : half * 128 + 128] for p in range(8)], axis=1
         )
         high = wide.astype(BF16)
         low = (wide - high.astype(F32)).astype(BF16)
-        gradient = dot(high, perm_ref[...]) + dot(low, perm_ref[...])
-        for k in range(8):
-            i = half * 8 + k
-            prior_ref[:, i * 8 : i * 8 + 8, :] = prior_ref[:, i * 8 : i * 8 + 8, :] + gradient[
-                :, k * 128 : k * 128 + 128
-            ].reshape(bands, 8, 128)
-
-    def update(b, carry):
-        out_ref[b] = (cube_ref[b].astype(F32) - step_ref[b] * prior_ref[b]).astype(BF16)
-        return carry
-
-    lax.fori_loop(0, bands, update, 0)
+        grows_ref[...] = dot(high, perm_ref[...]) + dot(low, perm_ref[...])
+        span = slice(half * 64, half * 64 + 64)
+
+        def update(b, carry):
+            at = pl.ds(pl.multiple_of(b * 8, 8), 8)
+            gradient = jnp.concatenate(
+                [grows_ref[at, k * 128 : k * 128 + 128] for k in range(8)], axis=0
+            )
+            total = gradient + prior_ref[b, span]
+            new_ref[b, span] = (cube_ref[b, span].astype(F32) - step_ref[b] * total).astype(BF16)
+            return carry
+
+        lax.fori_loop(0, bands, update, 0, unroll=4)
+        store = pltpu.make_async_copy(
+            new_ref.at[:, span], out_hbm.at[:, span], load_sem.at[3 + half]
+        )
+        store.start()
+        stores.append(store)
+    for store in stores:
+        store.wait()
     for copy in res_copies:
         copy.wait()
 
@@ -333,9 +359,13 @@
             jax.ShapeDtypeStruct(image.shape, F32),
         ),
         in_specs=[hbm, hbm, vmem, hbm if direct else vmem] + [smem] * 4,
-        out_specs=(vmem, vmem),
+        out_specs=(hbm, vmem),
         scratch_shapes=[
             pltpu.VMEM(cube.shape, BF16),
+            pltpu.VMEM(cube.shape, BF16),
+            pltpu.VMEM((rows, 1024), F32),
+            pltpu.VMEM((512, 384), BF16),
+            pltpu.VMEM((1024, 384), F32),
             pltpu.VMEM(kernels.shape, BF16),
             pltpu.VMEM((height // BLOCK, BLOCK, width), F32),
             pltpu.VMEM((height // BLOCK, BLOCK, width), F32),
@@ -353,12 +383,12 @@
             pltpu.VMEM((2 * PIX, 128), F32),
             pltpu.VMEM((2 * PIX, 128), F32),
             pltpu.VMEM((2 * PIX, 128), F32),
-            pltpu.SemaphoreType.DMA((3,)),
+            pltpu.SemaphoreType.DMA((5,)),
             pltpu.SemaphoreType.DMA((sems,)),
             pltpu.SemaphoreType.DMA((sems,)),
         ],
         compiler_params=pltpu.CompilerParams(
-            collective_id=0, has_side_effects=True, vmem_limit_bytes=50 << 20
+            collective_id=0, has_side_effects=True, vmem_limit_bytes=62 << 20
         ),
     )(cube, kernels, zone_map, image, kernel_index.T, step_size, spectral_weight, prior_taps)
     if direct:

time: 32.2 us -> 25.7 us (0.80)
  local copies, waits for them, and re-layouts: 7.51 us -> 2.93 us
  Pallas kernels: 23.7 us -> 22 us
    unnamed x18 -> x4, local copies, waits for them, and re-layouts: 7.51 us -> 2.93 us
    pallas_call x1, Pallas kernels: 23.7 us -> 22 us  [per_device(): pl.pallas_call(functools.partial(kernel, tiles, direct), out_shape=(jax.S...]
where the time goes in v2:
time: 25.7 us; the launch traced here: 25.6 us
  Pallas kernels  22 us (86%)
  local copies, waits for them, and re-layouts  2.93 us (11%)
  between operations  0.65 us (3%)
    pallas_call x1, Pallas kernels, per_device(): pl.pallas_call(functools.partial(kernel, tiles, direct), out_shape=(jax.S...  22 us
    unnamed x4, local copies, waits for them, and re-layouts  2.93 us

profile of v2, /device:TPU:0, one launch (start us, length us, event | category | flops | bytes accessed | tf_op | source)
XLA Modules:
  0.0 25.6 jit_solution(14275382924818426805)
XLA Ops:
  0.6 22.0 %shard_map.95 = (bf16[32,128,128]{2,1,0:T(8,128)(2,1)}, f32[8,1024]{1,0:T(8,128)}) custom-call(bf16[32,128,128]{2,1,0:T(8,128)(2,1)} %cube_hbm.1, bf16[32,64,192]{2,1,0:T(8,128)(2,1)} %kern_hbm.1, s32[16,16]{1,0:T(8,128)} %zone_ref.1, f32[8,1024]{1,0:T(8,128)} %meas_ref.1, s32[4,64]{1,0:T(4,128)} %bitcast.1, f32[32]{0:T(128)} %step_ref.1, f32[32]{0:T(128)} %weight_ref.1, ...), custom_call_target="tpu_custom_call" | custom-call | tf_op jit(solution)/shard_map/pallas_call | solution.py:355
  22.6 0.0 copy-start
  22.6 2.3 %copy.12 = bf16[32,128,128]{2,1,0:T(8,128)(2,1)} copy(bf16[32,128,128]{2,1,0:T(8,128)(2,1)} %get-tuple-element.4) | data formatting | bytes 2097152
  24.9 0.0 copy-done
  24.9 0.6 %copy.13 = f32[8,1024]{1,0:T(8,128)} copy(f32[8,1024]{1,0:T(8,128)S(1)} %copy-done) | data formatting | bytes 65536
Async XLA Ops:
  22.6 2.3 %copy-start = (f32[8,1024]{1,0:T(8,128)S(1)}, f32[8,1024]{1,0:T(8,128)}, u32[]{:S(2)}) copy-start(f32[8,1024]{1,0:T(8,128)} %get-tuple-element.5) | copy-start | bytes 98308

commit v3 on v2

--- a/solution.py
+++ b/solution.py
@@ -80,33 +80,6 @@
             device_id=device, device_id_type=MESH,
         )
 
-    pl.semaphore_wait(barrier, len(greeted))
-    copies = [
-        remote(0, cube_hbm.at[(bands - 1) * (1 - h)], edge_ref, partner),
-        remote(1, hsend_ref, hrecv_ref.at[0], right),
-        remote(2, hsend_ref, hrecv_ref.at[1], left),
-        remote(3, mine_ref, theirs_ref, partner),
-    ]
-    copies[0].start()
-    meas_copies = [
-        remote(
-            3 + d,
-            meas_ref.at[:, pl.ds(pl.multiple_of(tile * 128, 128), 128)],
-            meas_blocks.at[me],
-            device,
-        )
-        for d, (tile, device) in enumerate(others, 1)
-    ]
-    for copy in meas_copies:
-        copy.start()
-    if direct:
-        load_own = pltpu.make_async_copy(
-            meas_ref.at[:, pl.ds(pl.multiple_of(t * 128, 128), 128)],
-            meas_blocks.at[me],
-            load_sem.at[2],
-        )
-        load_own.start()
-
     load_cube.wait()
     for pair in range(8):
         two = cube_ref[:, pair * 16 : pair * 16 + 16, :].astype(F32)
@@ -121,8 +94,34 @@
     wanted = (sel_lane // 2) * 128 + jnp.where(sel_lane % 2 == 0, 127, 0)
     hsend_ref[...] = dot(xcat_ref[...], onehot(sel_row == wanted)).astype(BF16)
 
+    pl.semaphore_wait(barrier, len(greeted))
+    copies = [
+        remote(0, cube_hbm.at[(bands - 1) * (1 - h)], edge_ref, partner),
+        remote(1, hsend_ref, hrecv_ref.at[0], right),
+        remote(2, hsend_ref, hrecv_ref.at[1], left),
+        remote(3, mine_ref, theirs_ref, partner),
+    ]
     copies[1].start()
     copies[2].start()
+    copies[0].start()
+    meas_copies = [
+        remote(
+            3 + d,
+            meas_ref.at[:, pl.ds(pl.multiple_of(tile * 128, 128), 128)],
+            meas_blocks.at[me],
+            device,
+        )
+        for d, (tile, device) in enumerate(others, 1)
+    ]
+    for copy in meas_copies:
+        copy.start()
+    if direct:
+        load_own = pltpu.make_async_copy(
+            meas_ref.at[:, pl.ds(pl.multiple_of(t * 128, 128), 128)],
+            meas_blocks.at[me],
+            load_sem.at[2],
+        )
+        load_own.start()
 
     for half in range(2):
         blocks = dot_nt(perm_ref[...], xcat_ref[:, half * 1024 : half * 1024 + 1024])

time: 25.7 us -> 25.5 us (level)
  Pallas kernels: 22 us -> 21.7 us
    pallas_call x1, Pallas kernels: 22 us -> 21.7 us  [per_device(): pl.pallas_call(functools.partial(kernel, tiles, direct), out_shape=(jax.S...]
where the time goes in v3:
time: 25.5 us; the launch traced here: 25.3 us
  Pallas kernels  21.7 us (85%)
  local copies, waits for them, and re-layouts  2.93 us (11%)
  between operations  0.65 us (3%)
    pallas_call x1, Pallas kernels, per_device(): pl.pallas_call(functools.partial(kernel, tiles, direct), out_shape=(jax.S...  21.7 us
    unnamed x4, local copies, waits for them, and re-layouts  2.93 us

profile of v3, /device:TPU:0, one launch (start us, length us, event | category | flops | bytes accessed | tf_op | source)
XLA Modules:
  0.0 25.3 jit_solution(9000076332260630358)
XLA Ops:
  0.6 21.7 %shard_map.95 = (bf16[32,128,128]{2,1,0:T(8,128)(2,1)}, f32[8,1024]{1,0:T(8,128)}) custom-call(bf16[32,128,128]{2,1,0:T(8,128)(2,1)} %cube_hbm.1, bf16[32,64,192]{2,1,0:T(8,128)(2,1)} %kern_hbm.1, s32[16,16]{1,0:T(8,128)} %zone_ref.1, f32[8,1024]{1,0:T(8,128)} %meas_ref.1, s32[4,64]{1,0:T(4,128)} %bitcast.1, f32[32]{0:T(128)} %step_ref.1, f32[32]{0:T(128)} %weight_ref.1, ...), custom_call_target="tpu_custom_call" | custom-call | tf_op jit(solution)/shard_map/pallas_call | solution.py:354
  22.3 0.0 copy-start
  22.3 2.3 %copy.12 = bf16[32,128,128]{2,1,0:T(8,128)(2,1)} copy(bf16[32,128,128]{2,1,0:T(8,128)(2,1)} %get-tuple-element.4) | data formatting | bytes 2097152
  24.6 0.0 copy-done
  24.7 0.6 %copy.13 = f32[8,1024]{1,0:T(8,128)} copy(f32[8,1024]{1,0:T(8,128)S(1)} %copy-done) | data formatting | bytes 65536
Async XLA Ops:
  22.3 2.3 %copy-start = (f32[8,1024]{1,0:T(8,128)S(1)}, f32[8,1024]{1,0:T(8,128)}, u32[]{:S(2)}) copy-start(f32[8,1024]{1,0:T(8,128)} %get-tuple-element.5) | copy-start | bytes 98308
